TPU v7x, 32 devices: a whole 2x2x4 slice. The times are simulated.
32 devices in a mesh: grp: 4 (over x, core), mem: 8 (over z, y).
Axes of the slice: x: 2, y: 2, z: 4, core: 2. Of those that a mesh axis runs over, the one named last changes fastest.
Arguments:
- leaf_fronts: float32 [4, 4096, 4096], P('grp', None, 'mem'), as said below
- block_owner: int32 [4, 32], P('grp', 'mem'), may hold values from 0 to 31, as said below
- root_front: float32 [4096, 4096], P('grp', 'mem'), as said below
Outputs:
- root_factor: float32 [4096, 4096], P('grp', 'mem')
- log_det: float32 [5], replicated
Inputs may be any that keep to these rules, and one draw needn't show every extreme that they name: Each row of block_owner is a permutation of 0 to 31. For each g, the matrix whose column block block_owner[g, t] is column block t of leaf_fronts[g] is symmetric positive definite. root_front is symmetric positive definite.
All inputs are finite; a program needn't handle non-finite values.
Results may differ from a plain program's by a relative error of at most 0.0021.
Values may be sent and summed in bfloat16 or wider, within the bound.
No kernel may reach another device: no remote copies, remote signals or barrier semaphores. Data moves between devices by JAX's collectives and lax.ppermute only.
A program may use at most 64 MiB of HBM per device.

v0:
```python
import jax
import jax.numpy as jnp
from jax import lax
from jax.sharding import PartitionSpec as P

PL = 3
PR = 2


def broadcast(value, axis, root):
    mine = lax.axis_index(axis) == root
    return lax.psum(jnp.where(mine, value, jnp.zeros_like(value)), axis)


def factor_panel(column, diagonal_block, holder, first_row, row_ids):
    eye_block = jnp.eye(diagonal_block.shape[0], dtype=jnp.float32)
    factor = jnp.linalg.cholesky(jnp.where(holder, diagonal_block, eye_block))
    panel_rows = lax.linalg.triangular_solve(
        factor, column, left_side=False, lower=True, transpose_a=True
    )
    panel_rows = jnp.where((row_ids >= first_row)[:, None], panel_rows, jnp.zeros_like(panel_rows))
    log_sum = 2.0 * jnp.sum(jnp.log(jnp.diagonal(factor)))
    return (panel_rows, log_sum)


def local(leaf_fronts, block_owner, root_front):
    members = lax.axis_size("mem")
    groups = lax.axis_size("grp")
    member = lax.axis_index("mem")
    my_group = lax.axis_index("grp")
    leaf_local = leaf_fronts[0]
    front_order = leaf_local.shape[0]
    owner_local = block_owner[0]
    per_member = owner_local.shape[0]
    block_width = front_order // (per_member * members)
    block_count = front_order // block_width
    cols_local = per_member * block_width
    owner_full = lax.all_gather(block_owner, "mem", axis=1, tiled=True)[0]
    slot_ids = jnp.arange(block_count, dtype=jnp.int32)
    row_ids = jnp.arange(front_order, dtype=jnp.int32)
    blocks = leaf_local.reshape(front_order, per_member, block_width)
    leaf_logs = jnp.zeros((), jnp.float32)
    for section_index in range(PL):
        holds_block = owner_local == section_index
        holder = jnp.any(holds_block)
        column = jnp.sum(jnp.where(holds_block[None, :, None], blocks, 0.0), axis=1)
        diagonal_block = column[section_index * block_width : (section_index + 1) * block_width]
        panel_rows, log_sum = factor_panel(
            column, diagonal_block, holder, section_index * block_width, row_ids
        )
        leaf_logs = leaf_logs + jnp.where(holder, log_sum, 0.0)
        source = jnp.sum(jnp.where(owner_full == section_index, slot_ids, 0)) // per_member
        shared = broadcast(panel_rows.astype(jnp.bfloat16), "mem", source)
        across = jnp.take(
            shared.reshape(block_count, block_width, block_width), owner_local, axis=0
        )
        blocks = blocks - jnp.einsum(
            "rc,jbc->rjb", shared, across, preferred_element_type=jnp.float32
        )
    keep_cols = owner_local >= PL
    masked = jnp.where(keep_cols[None, :, None], blocks, 0.0).reshape(
        block_count, block_width, cols_local
    )
    quarter_rows = root_front.shape[0]
    root_logs = jnp.zeros((), jnp.float32)
    placed_front = lax.dynamic_update_slice_in_dim(
        jnp.zeros((front_order, cols_local), jnp.float32), root_front, my_group * quarter_rows, 0
    )
    taken = jnp.take(masked, owner_full, axis=0)
    placed = jnp.where((owner_full >= PL)[:, None, None], taken, 0.0)
    root_full = lax.psum(placed.reshape(front_order, cols_local) + placed_front, "grp")
    panels_full = jnp.zeros_like(root_full)
    for section_index in range(PR):
        owner_member, local_slot = divmod(section_index, per_member)
        column = root_full[:, local_slot * block_width : (local_slot + 1) * block_width]
        diagonal_block = column[section_index * block_width : (section_index + 1) * block_width]
        holder = member == owner_member
        panel_rows, log_sum = factor_panel(
            column, diagonal_block, holder, section_index * block_width, row_ids
        )
        root_logs = root_logs + jnp.where(holder & (my_group == 0), log_sum, 0.0)
        full_panel = broadcast(panel_rows.astype(jnp.bfloat16), "mem", owner_member)
        col_rows = lax.dynamic_slice_in_dim(full_panel, member * cols_local, cols_local, 0)
        root_full = root_full - jnp.einsum(
            "rc,xc->rx", full_panel, col_rows, preferred_element_type=jnp.float32
        )
        kept_block = panels_full[:, local_slot * block_width : (local_slot + 1) * block_width]
        panels_full = panels_full.at[
            :, local_slot * block_width : (local_slot + 1) * block_width
        ].set(jnp.where(holder, panel_rows, kept_block))
    root_local = lax.dynamic_slice_in_dim(root_full, my_group * quarter_rows, quarter_rows, 0)
    panels_kept = lax.dynamic_slice_in_dim(panels_full, my_group * quarter_rows, quarter_rows, 0)
    global_rows = my_group * quarter_rows + jnp.arange(quarter_rows, dtype=jnp.int32)
    column_blocks = member * per_member + jnp.arange(per_member, dtype=jnp.int32)
    pivot_cols = jnp.repeat(column_blocks < PR, block_width, total_repeat_length=cols_local)
    trailing = jnp.where((global_rows >= PR * block_width)[:, None], root_local, 0.0)
    root_factor = jnp.where(pivot_cols[None, :], panels_kept, trailing)
    places = jnp.arange(groups + 1, dtype=jnp.int32)
    terms = jnp.where(places == my_group, leaf_logs / (PL * block_width), 0.0) + jnp.where(
        places == groups, root_logs / (PR * block_width), 0.0
    )
    log_det = lax.psum(terms, ("grp", "mem"))
    return (root_factor, log_det)


def solution(mesh):
    in_specs = (P("grp", None, "mem"), P("grp", "mem"), P("grp", "mem"))
    out_specs = (P("grp", "mem"), P())
    return jax.shard_map(local, mesh=mesh, in_specs=in_specs, out_specs=out_specs, check_vma=False)
```

profile of v0, /device:TPU:0, one launch (start us, length us, event | category | flops | bytes accessed | tf_op | source)
XLA Modules:
  0.0 842.2 jit_solution(10672149471551786729)
XLA Ops:
  9.9 13.1 %all-reduce.1 = s32[32]{0:T(128)S(1)} all-reduce(s32[32]{0:T(128)S(1)} %get-tuple-element.74), channel_id=1, replica_groups=mesh['grp'=4,'mem'=8] {'mem'}, use_global_device_ids=true, to_apply=%add.1 | all-reduce | flops 32 | bytes 256 | tf_op jit(solution)/shard_map/squeeze | solution.py:38
  27.6 8.9 %copy.38 = f32[1,4096,512]{1,2,0:T(8,128)} copy(f32[1,4096,512]{2,1,0:T(8,128)} %param.14) | data formatting | bytes 16777216 | tf_op args[0]
  36.6 8.9 %copy.44 = f32[4096,4,128]{2,0,1:T(8,128)} copy(f32[4096,4,128]{0,2,1:T(8,128)} %bitcast.141) | data formatting | bytes 16777216 | tf_op jit(solution)/shard_map/reshape;squeeze | solution.py:41
  51.4 11.7 %cholesky.89 = f32[128,128]{1,0:T(8,128)S(1)} custom-call(f32[128,128]{1,0:T(8,128)S(1)} %fusion.34), custom_call_target="Cholesky" | custom-call | tf_op jit(solution)/shard_map/jit(cholesky)/cholesky | solution.py:17
  64.4 9.8 %custom-call.19 = f32[1,128,128]{1,2,0:T(8,128)S(1)} custom-call(f32[1,128,128]{2,1,0:T(8,128)S(1)} %get-tuple-element.61), custom_call_target="InvertDiagBlocksLowerTriangular" | custom-call | tf_op jit(solution)/shard_map/triangular_solve/custom-call.0 | solution.py:18
  79.8 73.8 %all-reduce.9.cloned.1.call-done = bf16[4096,128]{0,1:T(8,128)(2,1)} async-done(((bf16[4096,128]{0,1:T(8,128)(2,1)}), bf16[4096,128]{0,1:T(8,128)(2,1)}) %all-reduce.9.cloned.1.call-update) | async-done | bytes 1048592 | tf_op jit(solution)/shard_map/psum | solution.py:12
  155.8 8.8 %select_reduce_fusion.1 = (f32[4096,128]{1,0:T(8,128)S(1)}, f32[4096,4,128]{2,0,1:T(8,128)}) fusion(pred[4]{0:T(512)(128)(4,1)S(1)} %get-tuple-element.71, f32[4096,4,128]{2,0,1:T(8,128)} %copy.44, bf16[4,128,128]{2,1,0:T(8,128)(2,1)S(1)} %gather_fusion.6, pred[4]{0:T(512)(128)(4,1)S(1)} %get-tuple-element.72, ...), kind=kOutput, calls=%fused_computation.12 | convolution fusion | flops 542703616 | bytes 20054024 | tf_op jit(solution)/shard_map/rc,jbc->rjb/dot_general | solution.py:57
  166.0 11.7 %cholesky.100 = f32[128,128]{1,0:T(8,128)S(1)} custom-call(f32[128,128]{1,0:T(8,128)S(1)} %fusion.32), custom_call_target="Cholesky" | custom-call | tf_op jit(solution)/shard_map/jit(cholesky)/cholesky | solution.py:17
  179.0 9.8 %custom-call.20 = f32[1,128,128]{1,2,0:T(8,128)S(1)} custom-call(f32[1,128,128]{2,1,0:T(8,128)S(1)} %get-tuple-element.59), custom_call_target="InvertDiagBlocksLowerTriangular" | custom-call | tf_op jit(solution)/shard_map/triangular_solve/custom-call.0 | solution.py:18
  194.8 74.7 %all-reduce.11.cloned.1.call-done = bf16[4096,128]{0,1:T(8,128)(2,1)} async-done(((bf16[4096,128]{0,1:T(8,128)(2,1)}), bf16[4096,128]{0,1:T(8,128)(2,1)}) %all-reduce.11.cloned.1.call-update) | async-done | bytes 1048592 | tf_op jit(solution)/shard_map/psum | solution.py:12
  282.1 11.7 %cholesky.111 = f32[128,128]{1,0:T(8,128)S(1)} custom-call(f32[128,128]{1,0:T(8,128)S(1)} %fusion.30), custom_call_target="Cholesky" | custom-call | tf_op jit(solution)/shard_map/jit(cholesky)/cholesky | solution.py:17
  295.1 9.8 %custom-call.21 = f32[1,128,128]{1,2,0:T(8,128)S(1)} custom-call(f32[1,128,128]{2,1,0:T(8,128)S(1)} %get-tuple-element.57), custom_call_target="InvertDiagBlocksLowerTriangular" | custom-call | tf_op jit(solution)/shard_map/triangular_solve/custom-call.0 | solution.py:18
  310.2 75.5 %all-reduce.13.cloned.1.call-done = bf16[4096,128]{0,1:T(8,128)(2,1)} async-done(((bf16[4096,128]{0,1:T(8,128)(2,1)}), bf16[4096,128]{0,1:T(8,128)(2,1)}) %all-reduce.13.cloned.1.call-update) | async-done | bytes 1048592 | tf_op jit(solution)/shard_map/psum | solution.py:12
  393.5 18.6 %copy.73 = f32[4096,4,128]{2,1,0:T(4,128)} copy(f32[4096,4,128]{2,0,1:T(8,128)S(1)} %subtract_select_fusion) | data formatting | bytes 16777216 | tf_op jit(solution)/shard_map/reshape | solution.py:61
  412.1 10.3 %reshape.387 = f32[32,128,512]{2,1,0:T(8,128)} reshape(f32[4096,4,128]{2,1,0:T(4,128)} %copy.73) | data formatting | bytes 16777216 | tf_op jit(solution)/shard_map/reshape | solution.py:61
  430.1 8.9 %copy.74 = f32[4096,512]{0,1:T(8,128)} copy(f32[4096,512]{1,0:T(8,128)} %bitcast.140) | data formatting | bytes 16777216 | tf_op jit(solution)/shard_map/jit(_take)/gather | solution.py:69
  465.0 138.2 %all-reduce.15.cloned.1.call-done = f32[4096,512]{0,1:T(8,128)} async-done(((f32[4096,512]{0,1:T(8,128)}), f32[4096,512]{0,1:T(8,128)}) %all-reduce.15.cloned.1.call-update) | async-done | bytes 8388624 | tf_op jit(solution)/shard_map/psum | solution.py:71
  605.0 11.7 %cholesky.122 = f32[128,128]{1,0:T(8,128)S(1)} custom-call(f32[128,128]{1,0:T(8,128)S(1)} %fusion.28), custom_call_target="Cholesky" | custom-call | tf_op jit(solution)/shard_map/jit(cholesky)/cholesky | solution.py:17
  618.0 9.8 %custom-call.22 = f32[1,128,128]{1,2,0:T(8,128)S(1)} custom-call(f32[1,128,128]{2,1,0:T(8,128)S(1)} %get-tuple-element.55), custom_call_target="InvertDiagBlocksLowerTriangular" | custom-call | tf_op jit(solution)/shard_map/triangular_solve/custom-call.0 | solution.py:18
  637.4 73.4 %all-reduce.17.cloned.1.call-done = bf16[4096,128]{0,1:T(8,128)(2,1)} async-done(((bf16[4096,128]{0,1:T(8,128)(2,1)}), bf16[4096,128]{0,1:T(8,128)(2,1)}) %all-reduce.17.cloned.1.call-update) | async-done | bytes 1048592 | tf_op jit(solution)/shard_map/psum | solution.py:12
  720.1 11.7 %cholesky.133 = f32[128,128]{1,0:T(8,128)S(1)} custom-call(f32[128,128]{1,0:T(8,128)S(1)} %fusion.26), custom_call_target="Cholesky" | custom-call | tf_op jit(solution)/shard_map/jit(cholesky)/cholesky | solution.py:17
  735.6 9.8 %custom-call.23 = f32[1,128,128]{1,2,0:T(8,128)S(1)} custom-call(f32[1,128,128]{2,1,0:T(8,128)S(1)} %get-tuple-element.53), custom_call_target="InvertDiagBlocksLowerTriangular" | custom-call | tf_op jit(solution)/shard_map/triangular_solve/custom-call.0 | solution.py:18
  755.9 40.0 %psum.55 = f32[5]{0:T(128)} all-reduce(f32[5]{0:T(128)S(1)} %fusion.61), channel_id=1, replica_groups=mesh['grp'=4,'mem'=8] {'grp','mem'}, use_global_device_ids=true, to_apply=%region_24.28 | all-reduce | flops 5 | bytes 40 | tf_op jit(solution)/shard_map/psum | solution.py:102
  798.0 30.0 %all-reduce.19.cloned.1.call-done = bf16[4096,128]{0,1:T(8,128)(2,1)} async-done(((bf16[4096,128]{0,1:T(8,128)(2,1)}), bf16[4096,128]{0,1:T(8,128)(2,1)}) %all-reduce.19.cloned.1.call-update) | async-done | bytes 1048592 | tf_op jit(solution)/shard_map/psum | solution.py:12
  (108 shorter events, 123.2 us)
Async XLA Ops:
  7.2 146.4 %all-reduce.9.cloned.1.call-start = ((), (), s32[]{:S(2)}) async-start(), calls=%async_computation | async-start | bytes 2097152 | tf_op jit(solution)/shard_map/psum | solution.py:12
  77.2 192.3 %all-reduce.11.cloned.1.call-start = ((), (), s32[]{:S(2)}) async-start(), calls=%async_computation.1 | async-start | bytes 2097152 | tf_op jit(solution)/shard_map/psum | solution.py:12
  191.8 193.9 %all-reduce.13.cloned.1.call-start = ((), (), s32[]{:S(2)}) async-start(), calls=%async_computation.2 | async-start | bytes 2097152 | tf_op jit(solution)/shard_map/psum | solution.py:12
  307.9 295.2 %all-reduce.15.cloned.1.call-start = ((), (), s32[]{:S(2)}) async-start(), calls=%async_computation.3 | async-start | bytes 16777216 | tf_op jit(solution)/shard_map/psum | solution.py:71
  450.6 260.2 %all-reduce.17.cloned.1.call-start = ((), (), s32[]{:S(2)}) async-start(), calls=%async_computation.4 | async-start | bytes 2097152 | tf_op jit(solution)/shard_map/psum | solution.py:12
  632.4 195.6 %all-reduce.19.cloned.1.call-start = ((), (), s32[]{:S(2)}) async-start(), calls=%async_computation.5 | async-start | bytes 2097152 | tf_op jit(solution)/shard_map/psum | solution.py:12
  715.9 3.2 copy-start
Sparse Core Ops, SparseCore 0:
  77.3 76.1 all-reduce.8
  191.9 77.5 all-reduce.10
  308.0 77.6 all-reduce.12
  450.7 152.4 all-reduce.14
  632.5 78.2 all-reduce.16
  750.2 77.7 all-reduce.18
where the time goes:
time: 851 us; the launch traced here: 842 us
  waiting for transfers between devices  466 us (55%)
  other arithmetic  153 us (18%)
  local copies, waits for them, and re-layouts  91.6 us (11%)
  blocking collectives  53 us (6%)
  matrix products  48.7 us (6%)
  between operations  28.3 us (3%)
    psum x5, waiting for transfers between devices, broadcast(): return lax.psum(jnp.where(mine, value, jnp.zeros_like(value)), axis)  327 us
    psum x1, waiting for transfers between devices, local(): lax.psum(placed.reshape(front_order, cols_local) + placed_front, 'grp')  138 us
    another operation x15, other arithmetic, factor_panel(): factor = jnp.linalg.cholesky(jnp.where(holder, diagonal_block, eye_block))  61.9 us
    another operation x10, other arithmetic, factor_panel(): lax.linalg.triangular_solve(factor, column, left_side=False, lower=True,...  52.3 us
    psum x1, blocking collectives, local(): log_det = lax.psum(terms, ('grp', 'mem'))  40 us
    reshape x2, local copies, waits for them, and re-layouts, local(): jnp.where(keep_cols[None, :, None], blocks, 0.0)  28.9 us
    dot_general x3, matrix products, local(): jnp.einsum('rc,jbc->rjb', shared, across, preferred_element_type=jnp.floa...  23.2 us
    another operation x5, matrix products, factor_panel(): lax.linalg.triangular_solve(factor, column, left_side=False, lower=True,...  18 us
  transfers between devices with their start and end apart: 6, of which 6 were waited for; matrix products, arithmetic and copies ran while one was open for 3% of the time, Pallas kernels for 0%

commit v1 on v0

--- a/solution.py
+++ b/solution.py
@@ -5,6 +5,11 @@
 
 PL = 3
 PR = 2
+
+
+def axis_by_axis(x, axis_one, axis_two):
+    half = lax.psum(x, axis_one)
+    return lax.psum(half, axis_two)
 
 
 def broadcast(value, axis, root):
@@ -99,7 +104,7 @@
     terms = jnp.where(places == my_group, leaf_logs / (PL * block_width), 0.0) + jnp.where(
         places == groups, root_logs / (PR * block_width), 0.0
     )
-    log_det = lax.psum(terms, ("grp", "mem"))
+    log_det = axis_by_axis(terms, "mem", "grp")
     return (root_factor, log_det)
 
 

time: 851 us -> 852 us (level)
  blocking collectives: 53 us -> 40 us
  waiting for transfers between devices: 466 us -> 479 us
    psum x1 -> x2, blocking collectives: 40 us -> 27 us  [the longest x1 20.8 us: axis_by_axis(): half = lax.psum(x, axis_one)]
    psum x1, waiting for transfers between devices: 138 us -> 150 us  [local(): lax.psum(placed.reshape(front_order, cols_local) + placed_front, 'grp')]
    unnamed x10 -> x12, local copies, waits for them, and re-layouts: 17.4 us -> 17.4 us
where the time goes in v1:
time: 852 us; the launch traced here: 843 us
  waiting for transfers between devices  479 us (56%)
  other arithmetic  154 us (18%)
  local copies, waits for them, and re-layouts  91.6 us (11%)
  matrix products  49.4 us (6%)
  blocking collectives  40 us (5%)
  between operations  28.3 us (3%)
    psum x5, waiting for transfers between devices, broadcast(): return lax.psum(jnp.where(mine, value, jnp.zeros_like(value)), axis)  328 us
    psum x1, waiting for transfers between devices, local(): lax.psum(placed.reshape(front_order, cols_local) + placed_front, 'grp')  150 us
    another operation x15, other arithmetic, factor_panel(): factor = jnp.linalg.cholesky(jnp.where(holder, diagonal_block, eye_block))  61.9 us
    another operation x10, other arithmetic, factor_panel(): lax.linalg.triangular_solve(factor, column, left_side=False, lower=True,...  52.3 us
    reshape x2, local copies, waits for them, and re-layouts, local(): jnp.where(keep_cols[None, :, None], blocks, 0.0)  28.9 us
    dot_general x3, matrix products, local(): jnp.einsum('rc,jbc->rjb', shared, across, preferred_element_type=jnp.floa...  23.2 us
    psum x1, blocking collectives, axis_by_axis(): half = lax.psum(x, axis_one)  20.8 us
    another operation x5, matrix products, factor_panel(): lax.linalg.triangular_solve(factor, column, left_side=False, lower=True,...  18.6 us
  transfers between devices with their start and end apart: 6, of which 6 were waited for; matrix products, arithmetic and copies ran while one was open for 3% of the time, Pallas kernels for 0%

profile of v1, /device:TPU:0, one launch (start us, length us, event | category | flops | bytes accessed | tf_op | source)
XLA Modules:
  0.0 843.3 jit_solution(11512504052918849375)
XLA Ops:
  9.9 13.1 %all-reduce.1 = s32[32]{0:T(128)S(1)} all-reduce(s32[32]{0:T(128)S(1)} %get-tuple-element.74), channel_id=1, replica_groups=mesh['grp'=4,'mem'=8] {'mem'}, use_global_device_ids=true, to_apply=%add.1 | all-reduce | flops 32 | bytes 256 | tf_op jit(solution)/shard_map/squeeze | solution.py:43
  27.6 8.9 %copy.38 = f32[1,4096,512]{1,2,0:T(8,128)} copy(f32[1,4096,512]{2,1,0:T(8,128)} %param.14) | data formatting | bytes 16777216 | tf_op args[0]
  36.6 8.9 %copy.44 = f32[4096,4,128]{2,0,1:T(8,128)} copy(f32[4096,4,128]{0,2,1:T(8,128)} %bitcast.141) | data formatting | bytes 16777216 | tf_op jit(solution)/shard_map/reshape;squeeze | solution.py:46
  51.4 11.7 %cholesky.89 = f32[128,128]{1,0:T(8,128)S(1)} custom-call(f32[128,128]{1,0:T(8,128)S(1)} %fusion.34), custom_call_target="Cholesky" | custom-call | tf_op jit(solution)/shard_map/jit(cholesky)/cholesky | solution.py:22
  64.4 9.8 %custom-call.19 = f32[1,128,128]{1,2,0:T(8,128)S(1)} custom-call(f32[1,128,128]{2,1,0:T(8,128)S(1)} %get-tuple-element.61), custom_call_target="InvertDiagBlocksLowerTriangular" | custom-call | tf_op jit(solution)/shard_map/triangular_solve/custom-call.0 | solution.py:23
  79.8 73.8 %all-reduce.9.cloned.1.call-done = bf16[4096,128]{0,1:T(8,128)(2,1)} async-done(((bf16[4096,128]{0,1:T(8,128)(2,1)}), bf16[4096,128]{0,1:T(8,128)(2,1)}) %all-reduce.9.cloned.1.call-update) | async-done | bytes 1048592 | tf_op jit(solution)/shard_map/psum | solution.py:17
  155.8 8.8 %select_reduce_fusion.1 = (f32[4096,128]{1,0:T(8,128)S(1)}, f32[4096,4,128]{2,0,1:T(8,128)}) fusion(pred[4]{0:T(512)(128)(4,1)S(1)} %get-tuple-element.71, f32[4096,4,128]{2,0,1:T(8,128)} %copy.44, bf16[4,128,128]{2,1,0:T(8,128)(2,1)S(1)} %gather_fusion.6, pred[4]{0:T(512)(128)(4,1)S(1)} %get-tuple-element.72, ...), kind=kOutput, calls=%fused_computation.12 | convolution fusion | flops 542703616 | bytes 20054024 | tf_op jit(solution)/shard_map/rc,jbc->rjb/dot_general | solution.py:62
  166.0 11.7 %cholesky.100 = f32[128,128]{1,0:T(8,128)S(1)} custom-call(f32[128,128]{1,0:T(8,128)S(1)} %fusion.32), custom_call_target="Cholesky" | custom-call | tf_op jit(solution)/shard_map/jit(cholesky)/cholesky | solution.py:22
  179.0 9.8 %custom-call.20 = f32[1,128,128]{1,2,0:T(8,128)S(1)} custom-call(f32[1,128,128]{2,1,0:T(8,128)S(1)} %get-tuple-element.59), custom_call_target="InvertDiagBlocksLowerTriangular" | custom-call | tf_op jit(solution)/shard_map/triangular_solve/custom-call.0 | solution.py:23
  194.8 74.7 %all-reduce.11.cloned.1.call-done = bf16[4096,128]{0,1:T(8,128)(2,1)} async-done(((bf16[4096,128]{0,1:T(8,128)(2,1)}), bf16[4096,128]{0,1:T(8,128)(2,1)}) %all-reduce.11.cloned.1.call-update) | async-done | bytes 1048592 | tf_op jit(solution)/shard_map/psum | solution.py:17
  282.1 11.7 %cholesky.111 = f32[128,128]{1,0:T(8,128)S(1)} custom-call(f32[128,128]{1,0:T(8,128)S(1)} %fusion.30), custom_call_target="Cholesky" | custom-call | tf_op jit(solution)/shard_map/jit(cholesky)/cholesky | solution.py:22
  295.1 9.8 %custom-call.21 = f32[1,128,128]{1,2,0:T(8,128)S(1)} custom-call(f32[1,128,128]{2,1,0:T(8,128)S(1)} %get-tuple-element.57), custom_call_target="InvertDiagBlocksLowerTriangular" | custom-call | tf_op jit(solution)/shard_map/triangular_solve/custom-call.0 | solution.py:23
  310.2 75.5 %all-reduce.13.cloned.1.call-done = bf16[4096,128]{0,1:T(8,128)(2,1)} async-done(((bf16[4096,128]{0,1:T(8,128)(2,1)}), bf16[4096,128]{0,1:T(8,128)(2,1)}) %all-reduce.13.cloned.1.call-update) | async-done | bytes 1048592 | tf_op jit(solution)/shard_map/psum | solution.py:17
  393.5 18.6 %copy.73 = f32[4096,4,128]{2,1,0:T(4,128)} copy(f32[4096,4,128]{2,0,1:T(8,128)S(1)} %subtract_select_fusion) | data formatting | bytes 16777216 | tf_op jit(solution)/shard_map/reshape | solution.py:66
  412.1 10.3 %reshape.387 = f32[32,128,512]{2,1,0:T(8,128)} reshape(f32[4096,4,128]{2,1,0:T(4,128)} %copy.73) | data formatting | bytes 16777216 | tf_op jit(solution)/shard_map/reshape | solution.py:66
  430.1 8.9 %copy.74 = f32[4096,512]{0,1:T(8,128)} copy(f32[4096,512]{1,0:T(8,128)} %bitcast.140) | data formatting | bytes 16777216 | tf_op jit(solution)/shard_map/jit(_take)/gather | solution.py:74
  452.7 150.4 %all-reduce.15.cloned.1.call-done = f32[4096,512]{0,1:T(8,128)} async-done(((f32[4096,512]{0,1:T(8,128)}), f32[4096,512]{0,1:T(8,128)}) %all-reduce.15.cloned.1.call-update) | async-done | bytes 8388624 | tf_op jit(solution)/shard_map/psum | solution.py:76
  605.0 11.7 %cholesky.122 = f32[128,128]{1,0:T(8,128)S(1)} custom-call(f32[128,128]{1,0:T(8,128)S(1)} %fusion.28), custom_call_target="Cholesky" | custom-call | tf_op jit(solution)/shard_map/jit(cholesky)/cholesky | solution.py:22
  618.0 9.8 %custom-call.22 = f32[1,128,128]{1,2,0:T(8,128)S(1)} custom-call(f32[1,128,128]{2,1,0:T(8,128)S(1)} %get-tuple-element.55), custom_call_target="InvertDiagBlocksLowerTriangular" | custom-call | tf_op jit(solution)/shard_map/triangular_solve/custom-call.0 | solution.py:23
  647.6 63.2 %all-reduce.17.cloned.1.call-done = bf16[4096,128]{0,1:T(8,128)(2,1)} async-done(((bf16[4096,128]{0,1:T(8,128)(2,1)}), bf16[4096,128]{0,1:T(8,128)(2,1)}) %all-reduce.17.cloned.1.call-update) | async-done | bytes 1048592 | tf_op jit(solution)/shard_map/psum | solution.py:17
  720.1 11.7 %cholesky.133 = f32[128,128]{1,0:T(8,128)S(1)} custom-call(f32[128,128]{1,0:T(8,128)S(1)} %fusion.26), custom_call_target="Cholesky" | custom-call | tf_op jit(solution)/shard_map/jit(cholesky)/cholesky | solution.py:22
  735.7 9.8 %custom-call.23 = f32[1,128,128]{1,2,0:T(8,128)S(1)} custom-call(f32[1,128,128]{2,1,0:T(8,128)S(1)} %get-tuple-element.53), custom_call_target="InvertDiagBlocksLowerTriangular" | custom-call | tf_op jit(solution)/shard_map/triangular_solve/custom-call.0 | solution.py:23
  753.0 20.8 %psum.62 = f32[5]{0:T(128)S(1)} all-reduce(f32[5]{0:T(128)S(1)} %fusion.61), channel_id=1, replica_groups=mesh['grp'=4,'mem'=8] {'mem'}, use_global_device_ids=true, to_apply=%region_24.28 | all-reduce | flops 5 | bytes 40 | tf_op jit(solution)/shard_map/psum | solution.py:11
  787.9 41.2 %all-reduce.19.cloned.1.call-done = bf16[4096,128]{0,1:T(8,128)(2,1)} async-done(((bf16[4096,128]{0,1:T(8,128)(2,1)}), bf16[4096,128]{0,1:T(8,128)(2,1)}) %all-reduce.19.cloned.1.call-update) | async-done | bytes 1048592 | tf_op jit(solution)/shard_map/psum | solution.py:17
  (111 shorter events, 130.1 us)
Async XLA Ops:
  7.2 146.4 %all-reduce.9.cloned.1.call-start = ((), (), s32[]{:S(2)}) async-start(), calls=%async_computation | async-start | bytes 2097152 | tf_op jit(solution)/shard_map/psum | solution.py:17
  77.2 192.3 %all-reduce.11.cloned.1.call-start = ((), (), s32[]{:S(2)}) async-start(), calls=%async_computation.1 | async-start | bytes 2097152 | tf_op jit(solution)/shard_map/psum | solution.py:17
  191.8 193.9 %all-reduce.13.cloned.1.call-start = ((), (), s32[]{:S(2)}) async-start(), calls=%async_computation.2 | async-start | bytes 2097152 | tf_op jit(solution)/shard_map/psum | solution.py:17
  307.9 295.2 %all-reduce.15.cloned.1.call-start = ((), (), s32[]{:S(2)}) async-start(), calls=%async_computation.3 | async-start | bytes 16777216 | tf_op jit(solution)/shard_map/psum | solution.py:76
  450.6 260.3 %all-reduce.17.cloned.1.call-start = ((), (), s32[]{:S(2)}) async-start(), calls=%async_computation.4 | async-start | bytes 2097152 | tf_op jit(solution)/shard_map/psum | solution.py:17
  632.4 196.6 %all-reduce.19.cloned.1.call-start = ((), (), s32[]{:S(2)}) async-start(), calls=%async_computation.5 | async-start | bytes 2097152 | tf_op jit(solution)/shard_map/psum | solution.py:17
  715.9 3.2 copy-start
  753.0 32.7 %copy-start.1 = (f32[4096,128]{0,1:T(8,128)S(1)}, f32[4096,128]{0,1:T(8,128)}, u32[]{:S(2)}) copy-start(f32[4096,128]{0,1:T(8,128)} %get-tuple-element.83) | copy-start | bytes 6291460
Sparse Core Ops, SparseCore 0:
  77.3 76.1 all-reduce.8
  191.9 77.5 all-reduce.10
  308.0 77.6 all-reduce.12
  450.7 152.4 all-reduce.14
  632.5 78.3 all-reduce.16
  750.9 78.0 all-reduce.18
